TPU v7x, 128 devices: a whole 4x4x4 slice. The times are simulated.
128 devices in a mesh: dp: 32 (over z, x, core), head: 4 (over y).
Axes of the slice: x: 4, y: 4, z: 4, core: 2. Of those that a mesh axis runs over, the one named last changes fastest.
Arguments:
- hidden: bfloat16 [1024, 2048], P('dp'), may hold values from -6 to 6
- attn_gain: float32 [2048], replicated, may hold values from 0.1 to 1.9
- w_query: bfloat16 [2048, 3072], P(None, 'head'), may hold values from -0.125 to 0.125
- w_latent: bfloat16 [2048, 576], P(None, 'head'), may hold values from -0.125 to 0.125
- latent_gain: float32 [512], replicated, may hold values from 0.1 to 1.9
- w_key_up: bfloat16 [16, 128, 512], P('head'), may hold values from -0.5 to 0.5
- w_value_up: bfloat16 [16, 512, 128], P('head'), may hold values from -0.25 to 0.25
- w_out: bfloat16 [2048, 2048], P('head'), may hold values from -0.125 to 0.125
- kv_cache: bfloat16 [1024, 128, 576], P('dp'), may hold values from -110 to 110
- lengths: int32 [1024], P('dp'), may hold values from 1 to 128, 65536 in all
- live_mask: int32 [1024], P('dp'), may hold values 0 or 1
- mlp_gain: float32 [2048], replicated, may hold values from 0.1 to 1.9
- w_router: bfloat16 [2048, 64], replicated, may hold values from -0.125 to 0.125
- routes: int32 [1024, 6], P('dp'), may hold values from 0 to 63, all different within a row; in each aligned block of 32 rows (0 to 31, 32 to 63, ...) at most 6 rows name the same one
- w_experts_in: bfloat16 [64, 2048, 2, 1408], P('dp', None, None, 'head'), may hold values from -0.125 to 0.125
- w_experts_out: bfloat16 [64, 1408, 2048], P('dp', 'head'), may hold values from -0.15625 to 0.15625
- w_shared_in: bfloat16 [2048, 2, 1408], P(None, None, 'head'), may hold values from -0.125 to 0.125
- w_shared_out: bfloat16 [1408, 2048], P('head'), may hold values from -0.15625 to 0.15625
Outputs:
- output: bfloat16 [1024, 2048], P('dp', 'head')
Inputs may be any that keep to these rules, and one draw needn't show every extreme that they name: Among the routes of one device's 32 rows no expert is named more than 6 times, a bound that some block reaches. Request t has cached positions 0 to lengths[t] - 1; some request has 128.
All inputs are finite; a program needn't handle non-finite values. No bound on the sum of `lengths` or of `live_mask` on one device may be relied on, other than what follows from the above.
Results may differ from a plain program's by a relative error of at most 0.02.
The roundings to bfloat16 on the way count: a program that leaves them out, or rounds other values in their place, can miss the bound.
Values may be sent and summed in bfloat16 or wider, within the bound.
A program may use at most 128 MiB of HBM per device.

v0:
```python
import math
import jax
import jax.numpy as jnp
from jax import lax
from jax.sharding import PartitionSpec as P

NOPE = 128
ROPE = 64
VDIM = 128
LAT = 512
norm_eps = 1e-06
rope_theta = 50000.0
route_scale = 2.446


def rms_norm(values, weights):
    mean_square = jnp.mean(values * values, axis=-1, keepdims=True)
    return values * lax.rsqrt(mean_square + norm_eps) * weights


def rotary(values, positions):
    half_size = values.shape[-1] // 2
    frequency = rope_theta ** (-jnp.arange(half_size, dtype=jnp.float32) / half_size)
    angles = positions.reshape((-1,) + (1,) * (values.ndim - 1)) * frequency
    first_half = values[..., :half_size]
    second_half = values[..., half_size:]
    cosine = jnp.cos(angles)
    sine_part = jnp.sin(angles)
    return jnp.concatenate(
        [
            first_half * cosine - second_half * sine_part,
            second_half * cosine + first_half * sine_part,
        ],
        axis=-1,
    )


def body(
    hidden,
    attn_gain,
    w_query,
    w_latent,
    latent_gain,
    w_key_up,
    w_value_up,
    w_out,
    kv_cache,
    lengths,
    live_mask,
    mlp_gain,
    w_router,
    routes,
    w_experts_in,
    w_experts_out,
    w_shared_in,
    w_shared_out,
):
    request_count = hidden.shape[0]
    model_width = hidden.shape[1]
    local_heads = w_key_up.shape[0]
    cache_length = kv_cache.shape[1]
    head_count = lax.axis_size("head")
    share_width = model_width // head_count
    column_start = lax.axis_index("head") * share_width
    dp_count = lax.axis_size("dp")
    local_experts = w_experts_in.shape[0]
    expert_total = local_experts * dp_count
    top_count = routes.shape[1]
    capacity = max(2, 2 * top_count * request_count // expert_total)
    normed = rms_norm(hidden.astype(jnp.float32), attn_gain).astype(jnp.bfloat16)
    query_all = jnp.dot(normed, w_query, preferred_element_type=jnp.float32).reshape(
        request_count, local_heads, NOPE + ROPE
    )
    positions = lengths.astype(jnp.float32)
    query_nope = query_all[..., :NOPE].astype(jnp.bfloat16)
    query_rope = rotary(query_all[..., NOPE:], positions).astype(jnp.bfloat16)
    query_latent = jnp.einsum(
        "rhn,hnc->rhc", query_nope, w_key_up, preferred_element_type=jnp.float32
    ).astype(jnp.bfloat16)
    fresh_part = jnp.dot(normed, w_latent, preferred_element_type=jnp.float32).astype(jnp.bfloat16)
    fresh_kv = lax.all_gather(fresh_part, "head", axis=1, tiled=True)
    latent_new = rms_norm(fresh_kv[:, :LAT].astype(jnp.float32), latent_gain)
    rope_new = rotary(fresh_kv[:, LAT:].astype(jnp.float32), positions)
    key_new = jnp.concatenate([latent_new, rope_new], axis=-1).astype(jnp.bfloat16)
    query_full = jnp.concatenate([query_latent, query_rope], axis=-1)
    inverse_root = 1.0 / math.sqrt(NOPE + ROPE)
    scores = (
        jnp.einsum("rhc,rjc->rhj", query_full, kv_cache, preferred_element_type=jnp.float32)
        * inverse_root
    )
    in_cache = jnp.arange(cache_length, dtype=jnp.int32)[None, :] < lengths[:, None]
    scores = jnp.where(in_cache[:, None, :], scores, -jnp.inf)
    score_new = (
        jnp.einsum("rhc,rc->rh", query_full, key_new, preferred_element_type=jnp.float32)
        * inverse_root
    )
    highest = jnp.maximum(jnp.max(scores, axis=-1), score_new)
    weights_cached = jnp.exp(scores - highest[..., None])
    weight_new = jnp.exp(score_new - highest)
    denominator = jnp.sum(weights_cached, axis=-1) + weight_new
    probabilities = (weights_cached / denominator[..., None]).astype(jnp.bfloat16)
    prob_new = (weight_new / denominator).astype(jnp.bfloat16)
    context = jnp.einsum(
        "rhj,rjc->rhc", probabilities, kv_cache[..., :LAT], preferred_element_type=jnp.float32
    )
    context = (
        context
        + prob_new.astype(jnp.float32)[..., None] * key_new[:, None, :LAT].astype(jnp.float32)
    ).astype(jnp.bfloat16)
    values = jnp.einsum(
        "rhc,hcv->rhv", context, w_value_up, preferred_element_type=jnp.float32
    ).astype(jnp.bfloat16)
    partial_value = jnp.dot(
        values.reshape(request_count, local_heads * VDIM), w_out, preferred_element_type=jnp.float32
    )
    attention = lax.psum(partial_value.astype(jnp.bfloat16), "head").astype(jnp.float32)
    mixed_rows = (hidden.astype(jnp.float32) + attention).astype(jnp.bfloat16)
    ffn_input = rms_norm(mixed_rows.astype(jnp.float32), mlp_gain).astype(jnp.bfloat16)
    mixed_share = lax.dynamic_slice_in_dim(mixed_rows, column_start, share_width, 1)
    logits = jnp.dot(ffn_input, w_router, preferred_element_type=jnp.float32)
    chosen = jax.nn.sigmoid(jnp.take_along_axis(logits, routes, axis=1))
    route_weight = (
        route_scale
        * live_mask.astype(jnp.float32)[:, None]
        * chosen
        / jnp.sum(chosen, axis=1, keepdims=True)
    )
    pair_count = request_count * top_count
    flat_routes = routes.reshape(pair_count)
    live_pairs = jnp.repeat(live_mask, top_count)
    member = (
        (flat_routes[:, None] == jnp.arange(expert_total, dtype=jnp.int32)[None, :])
        & (live_pairs[:, None] == 1)
    ).astype(jnp.int32)
    earlier = jnp.cumsum(member, axis=0) - member
    slot_rank = jnp.sum(earlier * member, axis=1)
    slot_total = expert_total * capacity
    buffer_slot = jnp.where(live_pairs == 1, flat_routes * capacity + slot_rank, slot_total)
    token_of_pair = jnp.arange(pair_count, dtype=jnp.int32) // top_count
    spread = ffn_input[token_of_pair]
    packed = (
        jnp.zeros((slot_total, ffn_input.shape[1]), jnp.bfloat16)
        .at[buffer_slot]
        .set(spread, mode="drop")
    )
    arrived = lax.all_to_all(
        packed.reshape(dp_count, local_experts, capacity, ffn_input.shape[1]),
        "dp",
        split_axis=0,
        concat_axis=0,
        tiled=True,
    )
    gate_up = jnp.einsum(
        "secd,edkf->seckf", arrived, w_experts_in, preferred_element_type=jnp.float32
    )
    acting = (jax.nn.silu(gate_up[..., 0, :]) * gate_up[..., 1, :]).astype(jnp.bfloat16)
    expert_part = jnp.einsum(
        "secf,efd->secd", acting, w_experts_out, preferred_element_type=jnp.float32
    )
    expert_share = lax.psum_scatter(
        expert_part.astype(jnp.bfloat16), "head", scatter_dimension=3, tiled=True
    )
    returned = lax.all_to_all(expert_share, "dp", split_axis=0, concat_axis=0, tiled=True)
    returned_rows = returned.reshape(slot_total, share_width)
    pick_slot = jnp.minimum(buffer_slot, slot_total - 1)
    pair_rows = returned_rows[pick_slot].astype(jnp.float32)
    routed = jnp.sum(
        (route_weight.reshape(pair_count)[:, None] * pair_rows).reshape(
            request_count, top_count, share_width
        ),
        axis=1,
    )
    shared_width = w_shared_out.shape[0]
    shared_pair = jnp.dot(
        ffn_input,
        w_shared_in.reshape(model_width, 2 * shared_width),
        preferred_element_type=jnp.float32,
    ).reshape(request_count, 2, shared_width)
    shared_act = (jax.nn.silu(shared_pair[:, 0]) * shared_pair[:, 1]).astype(jnp.bfloat16)
    shared_part = jnp.dot(shared_act, w_shared_out, preferred_element_type=jnp.float32)
    shared_share = lax.psum_scatter(
        shared_part.astype(jnp.bfloat16), "head", scatter_dimension=1, tiled=True
    ).astype(jnp.float32)
    return (mixed_share.astype(jnp.float32) + shared_share + routed).astype(jnp.bfloat16)


def solution(mesh):
    placed = (
        P("dp", None),
        P(),
        P(None, "head"),
        P(None, "head"),
        P(),
        P("head", None, None),
        P("head", None, None),
        P("head", None),
        P("dp", None, None),
        P("dp"),
        P("dp"),
        P(),
        P(),
        P("dp", None),
        P("dp", None, None, "head"),
        P("dp", "head", None),
        P(None, None, "head"),
        P("head", None),
    )
    return jax.shard_map(
        body, mesh=mesh, in_specs=placed, out_specs=P("dp", "head"), check_vma=False
    )
```

profile of v0, /device:TPU:1, one launch (start us, length us, event | category | flops | bytes accessed | tf_op | source)
XLA Modules:
  0.0 187.7 jit_solution(8351223471823655975)
XLA Ops:
  6.6 0.8 convert_element_type.107
  7.4 0.9 iota_compare_fusion.2
  8.2 1.0 fusion.40
  9.3 1.5 fusion.29
  10.8 10.4 %all-gather = bf16[4,144,32]{1,2,0:T(8,128)(2,1)S(1)} all-gather(bf16[1,144,32]{1,2,0:T(8,128)(2,1)S(1)} %fusion.29), channel_id=1, replica_groups=mesh['dp'=32,'head'=4] {'head'}, dimensions={0}, use_global_device_ids=true | all-gather | bytes 46080 | tf_op jit(solution)/shard_map/all_gather | solution.py:81
  21.3 0.1 fusion.50
  21.5 1.6 fusion.61
  23.0 0.1 reshape.311
  23.4 1.2 fusion.26
  24.7 0.1 subtract_convert_fusion.1
  25.0 0.3 fusion.46
  25.3 3.4 %fusion.78 = (f32[32,4]{1,0:T(8,128)S(1)}, f32[32,4,128]{2,1,0:T(4,128)S(1)}) fusion(bf16[32,128,576]{1,2,0:T(8,128)(2,1)} %param.26, bf16[32,4,576]{2,0,1:T(8,128)(2,1)S(1)} %pad_maximum_fusion, pred[32,128]{1,0:T(8,128)(4,1)S(1)} %iota_compare_fusion.2), kind=kOutput, calls=%fused_computation.128 | convolution fusion | flops 18923392 | bytes 4936192 | tf_op jit(solution)/shard_map/rhc,rjc->rhj/dot_general | solution.py:88
  28.7 0.2 fusion.57
  28.9 0.1 copy-done.1
  29.1 1.2 fusion.23
  30.3 0.2 fusion.28
  30.6 0.3 copy-done.3
  30.8 1.1 convolution_convert_fusion.1
  32.1 0.1 eq.62
  32.2 0.1 eq.57
  32.8 0.6 reduce-window.6
  33.4 0.2 slice_reduce_fusion
  33.8 41.9 %all-reduce.3.cloned.1.call-done = bf16[32,2048]{1,0:T(8,128)(2,1)} async-done(((bf16[32,2048]{1,0:T(8,128)(2,1)}), bf16[32,2048]{1,0:T(8,128)(2,1)}) %all-reduce.3.cloned.1.call-update) | async-done | bytes 131088 | tf_op jit(solution)/shard_map/psum | solution.py:116
  75.7 1.1 fusion.37
  76.8 0.6 copy-done.5
  77.5 5.6 %scatter_custom_fusion = bf16[384,2048]{1,0:T(8,128)(2,1)} fusion(s32[192]{0:T(256)S(1)} %bitcast.114, bf16[32,2048]{1,0:T(8,128)(2,1)S(1)} %fusion.39, s32[1024]{0:T(1024)S(1)} %pad_clamp_fusion.1, bf16[]{:T(256)} %constant.75.clone.1), kind=kCustom, calls=%fused_computation.28 | custom fusion | bytes 1572866 | tf_op jit(solution)/shard_map/scatter | solution.py:144
  83.1 3.7 %reshape.317 = bf16[32,2,6,2048]{3,2,1,0:T(8,128)(2,1)} reshape(bf16[384,2048]{1,0:T(8,128)(2,1)} %scatter_custom_fusion) | data formatting | bytes 3145728 | tf_op jit(solution)/shard_map/reshape | solution.py:147
  86.8 3.2 %copy.96 = bf16[32,2,6,2048]{3,1,2,0:T(2,128)(2,1)S(1)} copy(bf16[32,2,6,2048]{3,2,1,0:T(8,128)(2,1)} %reshape.317) | data formatting | bytes 3145728 | tf_op jit(solution)/shard_map/reshape | solution.py:147
  90.0 32.3 %all_to_all.10 = bf16[32,2,6,2048]{3,1,2,0:T(2,128)(2,1)S(1)} all-to-all(bf16[32,2,6,2048]{3,1,2,0:T(2,128)(2,1)S(1)} %copy.96), channel_id=1, replica_groups=mesh['dp'=32,'head'=4] {'dp'}, dimensions={0} | all-to-all | bytes 3145728 | tf_op jit(solution)/shard_map/all_to_all | solution.py:146
  122.4 5.9 %fusion.15 = f32[32,2,6,2,352]{4,0,3,2,1:T(8,128)S(1)} fusion(bf16[2,2048,2,352]{1,3,2,0:T(8,128)(2,1)} %param.32, bf16[32,2,6,2048,1]{3,1,2,0,4:T(2,128)(2,1)S(1)} %bitcast.106), kind=kOutput, calls=%fused_computation.17 | convolution fusion | flops 1107296256 | bytes 8421376 | tf_op jit(solution)/shard_map/secd,edkf->seckf/dot_general | solution.py:153
  128.3 2.2 %fusion.11 = bf16[32,2,6,2048]{3,0,2,1:T(8,128)(2,1)} fusion(bf16[2,352,2048]{2,1,0:T(8,128)(2,1)S(1)} %copy-done.10, f32[32,2,6,2,352]{4,0,3,2,1:T(8,128)S(1)} %fusion.15), kind=kOutput, calls=%fused_computation.13 | convolution fusion | flops 555245568 | bytes 5537792 | tf_op jit(solution)/shard_map/secf,efd->secd/dot_general | solution.py:157
  130.7 0.6 pad_clamp_fusion
  131.3 1.1 fusion.79
  132.4 1.6 gather_fusion.1
  134.3 2.9 %fusion.6 = f32[32,2,352]{2,0,1:T(8,128)S(1)} fusion(bf16[2048,2,352]{0,2,1:T(8,128)(2,1)} %param.34, bf16[32,2048]{1,0:T(8,128)(2,1)S(1)} %fusion.39), kind=kOutput, calls=%fused_computation.10 | convolution fusion | flops 92274688 | bytes 3104768 | tf_op jit(solution)/shard_map/dot_general | solution.py:174
  137.2 1.0 convolution_convert_fusion
  138.3 13.7 %reduce-scatter.5.cloned.1.call-done = bf16[32,2,6,512]{3,0,2,1:T(8,128)(2,1)} async-done(((bf16[32,2,6,2048]{3,0,2,1:T(8,128)(2,1)}), bf16[32,2,6,512]{3,0,2,1:T(8,128)(2,1)}) %reduce-scatter.5.cloned.1.call-update) | async-done | bytes 393232 | tf_op jit(solution)/shard_map/reduce_scatter | solution.py:160
  151.9 2.1 %copy.99 = bf16[32,2,6,512]{3,1,2,0:T(2,128)(2,1)} copy(bf16[32,2,6,512]{3,0,2,1:T(8,128)(2,1)} %reduce-scatter.5.cloned.1.call-done) | data formatting | bytes 786432 | tf_op jit(solution)/shard_map/reduce_scatter | solution.py:160
  154.1 8.6 %all-to-all-start.1 = ((bf16[32,2,6,512]{3,1,2,0:T(2,128)(2,1)}), bf16[32,2,6,512]{3,1,2,0:T(2,128)(2,1)S(1)}, u32[]{:S(2)}, u32[]{:S(2)}) async-start(bf16[32,2,6,512]{3,1,2,0:T(2,128)(2,1)} %copy.99), calls=%async_computation.3 | async-start | bytes 786432 | tf_op jit(solution)/shard_map/all_to_all | solution.py:163
  162.7 0.6 multiply_divide_fusion
  163.3 0.8 copy.91
  164.0 8.8 %all-to-all-done.1 = bf16[32,2,6,512]{3,1,2,0:T(2,128)(2,1)S(1)} async-done(((bf16[32,2,6,512]{3,1,2,0:T(2,128)(2,1)}), bf16[32,2,6,512]{3,1,2,0:T(2,128)(2,1)S(1)}, u32[]{:S(2)}, u32[]{:S(2)}) %all-to-all-start.1) | async-done | bytes 393248 | tf_op jit(solution)/shard_map/all_to_all | solution.py:163
  172.8 0.9 copy.100
  173.7 1.2 reshape.318
  174.9 1.8 gather_fusion
  176.7 1.8 reshape.320
  178.4 1.3 multiply_reduce_fusion
  179.7 1.4 add_convert_fusion
  (67 shorter events, 2.0 us)
Async XLA Ops:
  6.5 14.9 %copy-start = (bf16[2048,768]{1,0:T(8,128)(2,1)S(1)}, bf16[2048,768]{1,0:T(8,128)(2,1)}, u32[]{:S(2)}) copy-start(bf16[2048,768]{1,0:T(8,128)(2,1)} %param.20) | copy-start | bytes 9437188
  6.5 69.2 %all-reduce.3.cloned.1.call-start = ((), (), s32[]{:S(2)}) async-start(), calls=%async_computation.4 | async-start | bytes 262144 | tf_op jit(solution)/shard_map/psum | solution.py:116
  21.2 2.2 %copy-start.9 = (f32[512]{0:T(512)S(1)}, f32[512]{0:T(512)}, u32[]{:S(2)}) copy-start(f32[512]{0:T(512)} %param.22) | copy-start | bytes 6148
  25.3 3.8 %copy-start.1 = (bf16[32,128,576]{1,2,0:T(8,128)(2,1)S(1)}, bf16[32,128,576]{1,2,0:T(8,128)(2,1)}, u32[]{:S(2)}) copy-start(bf16[32,128,576]{1,2,0:T(8,128)(2,1)} %param.26) | copy-start | bytes 14155780
  29.1 1.2 copy-start.6
  29.1 1.8 copy-start.3
  30.3 1.7 copy-start.11
  30.3 2.1 %copy-start.7 = (s32[32,6]{0,1:T(8,128)S(1)}, s32[32,6]{0,1:T(8,128)}, u32[]{:S(2)}) copy-start(s32[32,6]{0,1:T(8,128)} %param.31) | copy-start | bytes 2308
  30.3 45.4 %copy-start.2 = (bf16[32,2048]{1,0:T(8,128)(2,1)S(1)}, bf16[32,2048]{1,0:T(8,128)(2,1)}, u32[]{:S(2)}) copy-start(bf16[32,2048]{1,0:T(8,128)(2,1)} %param.18) | copy-start | bytes 393220
  30.3 47.1 %copy-start.8 = (f32[2048]{0:T(1024)S(1)}, f32[2048]{0:T(1024)}, u32[]{:S(2)}) copy-start(f32[2048]{0:T(1024)} %param.29) | copy-start | bytes 24580
  32.0 120.0 %reduce-scatter.5.cloned.1.call-start = ((), (), s32[]{:S(2)}) async-start(), calls=%async_computation.6 | async-start | bytes 1966080 | tf_op jit(solution)/shard_map/reduce_scatter | solution.py:160
  76.8 0.6 copy-start.5
  122.4 5.9 %copy-start.10 = (bf16[2,352,2048]{2,1,0:T(8,128)(2,1)S(1)}, bf16[2,352,2048]{2,1,0:T(8,128)(2,1)}, u32[]{:S(2)}) copy-start(bf16[2,352,2048]{2,1,0:T(8,128)(2,1)} %param.33) | copy-start | bytes 8650756
  130.4 49.3 %reduce-scatter.3.cloned.1.call-start = ((), (), s32[]{:S(2)}) async-start(), calls=%async_computation.5 | async-start | bytes 163840 | tf_op jit(solution)/shard_map/reduce_scatter | solution.py:181
  134.3 3.0 %copy-start.4 = (bf16[352,2048]{1,0:T(8,128)(2,1)S(1)}, bf16[352,2048]{1,0:T(8,128)(2,1)}, u32[]{:S(2)}) copy-start(bf16[352,2048]{1,0:T(8,128)(2,1)} %param.35) | copy-start | bytes 4325380
  154.1 18.7 %all-to-all-start.1 = ((bf16[32,2,6,512]{3,1,2,0:T(2,128)(2,1)}), bf16[32,2,6,512]{3,1,2,0:T(2,128)(2,1)S(1)}, u32[]{:S(2)}, u32[]{:S(2)}) async-start(bf16[32,2,6,512]{3,1,2,0:T(2,128)(2,1)} %copy.99), calls=%async_computation.3 | async-start | bytes 786432 | tf_op jit(solution)/shard_map/all_to_all | solution.py:163
Sparse Core Ops, SparseCore 0:
  32.1 43.5 all-reduce.2
  130.6 21.3 reduce-scatter.4
  154.4 19.3 reduce-scatter.2
where the time goes:
time: 188 us
  waiting for transfers between devices  64.4 us (34%)
  blocking collectives  42.7 us (23%)
  local copies, waits for them, and re-layouts  25.4 us (14%)
  matrix products  23.6 us (13%)
  between operations  13.4 us (7%)
  other arithmetic  9.43 us (5%)
  starting transfers between devices  8.64 us (5%)
    psum x1, waiting for transfers between devices, body(): lax.psum(partial_value.astype(jnp.bfloat16), 'head').astype(jnp.float32)  41.9 us
    all_to_all x1, blocking collectives, body(): lax.all_to_all(packed.reshape(dp_count, local_experts, capacity, ffn_inpu...  32.3 us
    reduce_scatter x1, waiting for transfers between devices, body(): lax.psum_scatter(expert_part.astype(jnp.bfloat16), 'head', scatter_dimens...  13.7 us
    all_gather x1, blocking collectives, body(): fresh_kv = lax.all_gather(fresh_part, 'head', axis=1, tiled=True)  10.4 us
    all_to_all x1, waiting for transfers between devices, body(): lax.all_to_all(expert_share, 'dp', split_axis=0, concat_axis=0, tiled=True)  8.77 us
    all_to_all x1, starting transfers between devices, body(): lax.all_to_all(expert_share, 'dp', split_axis=0, concat_axis=0, tiled=True)  8.56 us
    reshape x2, local copies, waits for them, and re-layouts, body(): packed.reshape(dp_count, local_experts, capacity, ffn_input.shape[1])  6.93 us
    dot_general x1, matrix products, body(): jnp.einsum('secd,edkf->seckf', arrived, w_experts_in, preferred_element_t...  5.86 us
  transfers between devices with their start and end apart: 4, of which 3 were waited for; matrix products, arithmetic and copies ran while one was open for 11% of the time, Pallas kernels for 0%

commit v1 on v0

--- a/solution.py
+++ b/solution.py
@@ -113,7 +113,9 @@
     partial_value = jnp.dot(
         values.reshape(request_count, local_heads * VDIM), w_out, preferred_element_type=jnp.float32
     )
-    attention = lax.psum(partial_value.astype(jnp.bfloat16), "head").astype(jnp.float32)
+    attention = jnp.sum(lax.all_gather(partial_value.astype(jnp.bfloat16), "head"), axis=0).astype(
+        jnp.float32
+    )
     mixed_rows = (hidden.astype(jnp.float32) + attention).astype(jnp.bfloat16)
     ffn_input = rms_norm(mixed_rows.astype(jnp.float32), mlp_gain).astype(jnp.bfloat16)
     mixed_share = lax.dynamic_slice_in_dim(mixed_rows, column_start, share_width, 1)

time: 188 us -> 172 us (0.915)
  waiting for transfers between devices: 64.4 us -> 22 us
  blocking collectives: 42.7 us -> 58.3 us
  other arithmetic: 9.43 us -> 18.7 us
  local copies, waits for them, and re-layouts: 25.4 us -> 27.4 us
    psum x1 -> x0, waiting for transfers between devices: 41.9 us -> none  [body(): lax.psum(partial_value.astype(jnp.bfloat16), 'head').astype(jnp.float32)]
    all_gather x0 -> x1, blocking collectives: none -> 10.6 us  [body(): lax.all_gather(partial_value.astype(jnp.bfloat16), 'head')]
    all_to_all x1, blocking collectives: 32.3 us -> 37.2 us  [body(): lax.all_to_all(packed.reshape(dp_count, local_experts, capacity, ffn_inpu...]
  transfers between devices with their start and end apart: 4 -> 3, of which waited for: 3 -> 2; matrix products, arithmetic and copies ran while one was open for 11% -> 11% of each run, Pallas kernels for 0% -> 0%
where the time goes in v1:
time: 172 us; the launch traced here: 171 us
  blocking collectives  58.3 us (34%)
  local copies, waits for them, and re-layouts  27.4 us (16%)
  matrix products  22.9 us (13%)
  waiting for transfers between devices  22 us (13%)
  other arithmetic  18.7 us (11%)
  between operations  13.7 us (8%)
  starting transfers between devices  8.49 us (5%)
    all_to_all x1, blocking collectives, body(): lax.all_to_all(packed.reshape(dp_count, local_experts, capacity, ffn_inpu...  37.2 us
    reduce_scatter x1, waiting for transfers between devices, body(): lax.psum_scatter(expert_part.astype(jnp.bfloat16), 'head', scatter_dimens...  14.4 us
    all_gather x1, blocking collectives, body(): lax.all_gather(partial_value.astype(jnp.bfloat16), 'head')  10.6 us
    all_gather x1, blocking collectives, body(): fresh_kv = lax.all_gather(fresh_part, 'head', axis=1, tiled=True)  10.4 us
    all_to_all x1, starting transfers between devices, body(): lax.all_to_all(expert_share, 'dp', split_axis=0, concat_axis=0, tiled=True)  8.45 us
    all_to_all x1, waiting for transfers between devices, body(): lax.all_to_all(expert_share, 'dp', split_axis=0, concat_axis=0, tiled=True)  7.53 us
    reshape x2, local copies, waits for them, and re-layouts, body(): packed.reshape(dp_count, local_experts, capacity, ffn_input.shape[1])  6.93 us
    dot_general x1, matrix products, body(): jnp.einsum('secd,edkf->seckf', arrived, w_experts_in, preferred_element_t...  5.86 us
  transfers between devices with their start and end apart: 3, of which 2 were waited for; matrix products, arithmetic and copies ran while one was open for 11% of the time, Pallas kernels for 0%

profile of v1, /device:TPU:1, one launch (start us, length us, event | category | flops | bytes accessed | tf_op | source)
XLA Modules:
  0.0 171.4 jit_solution(15776220244076970243)
XLA Ops:
  7.7 0.7 broadcast_compare_fusion
  8.4 0.7 eq.62
  9.1 0.7 eq.57
  9.8 1.2 convert_element_type.109
  11.0 0.7 iota_compare_fusion.2
  11.7 0.7 broadcast_multiply_fusion
  12.4 0.8 copy.93
  13.2 1.0 fusion.40
  14.2 1.5 fusion.29
  15.7 10.4 %all-gather.1 = bf16[4,144,32]{1,2,0:T(8,128)(2,1)S(1)} all-gather(bf16[1,144,32]{1,2,0:T(8,128)(2,1)S(1)} %fusion.29), channel_id=1, replica_groups=mesh['dp'=32,'head'=4] {'head'}, dimensions={0}, use_global_device_ids=true | all-gather | bytes 46080 | tf_op jit(solution)/shard_map/all_gather | solution.py:81
  26.3 0.7 fusion.50
  26.9 1.6 fusion.61
  28.8 1.3 pad_clamp_fusion.1
  30.2 0.7 mul.265
  30.9 0.7 fusion.56
  31.6 0.6 reduce-window.6
  32.6 0.7 fusion.54
  33.3 0.6 add_rsqrt_fusion.1
  33.9 0.8 fusion.75
  34.7 1.2 fusion.26
  35.9 0.8 subtract_convert_fusion.1
  37.2 3.4 %fusion.78 = (f32[32,4]{1,0:T(8,128)S(1)}, f32[32,4,128]{2,1,0:T(4,128)S(1)}) fusion(bf16[32,128,576]{1,2,0:T(8,128)(2,1)} %param.26, bf16[32,4,576]{2,0,1:T(8,128)(2,1)S(1)} %pad_maximum_fusion, pred[32,128]{1,0:T(8,128)(4,1)S(1)} %iota_compare_fusion.2), kind=kOutput, calls=%fused_computation.128 | convolution fusion | flops 18923392 | bytes 4936192 | tf_op jit(solution)/shard_map/rhc,rjc->rhj/dot_general | solution.py:88
  40.9 1.2 fusion.23
  43.2 10.6 %all-gather = bf16[128,2048]{1,0:T(8,128)(2,1)} all-gather(bf16[32,2048]{1,0:T(8,128)(2,1)S(1)} %convolution_convert_fusion.1), channel_id=2, replica_groups=mesh['dp'=32,'head'=4] {'head'}, dimensions={0}, use_global_device_ids=true | all-gather | bytes 655360 | tf_op jit(solution)/shard_map/all_gather | solution.py:116
  53.8 1.1 reduce_sum.80
  55.9 5.7 %scatter_custom_fusion = bf16[384,2048]{1,0:T(8,128)(2,1)} fusion(s32[192]{0:T(256)S(1)} %bitcast.117, bf16[32,2048]{1,0:T(8,128)(2,1)S(1)} %fusion.39, s32[1024]{0:T(1024)} %pad_clamp_fusion.1, bf16[]{:T(256)} %constant.23.clone.1), kind=kCustom, calls=%fused_computation.28 | custom fusion | bytes 1573376 | tf_op jit(solution)/shard_map/scatter | solution.py:146
  61.6 3.7 %reshape.317 = bf16[32,2,6,2048]{3,2,1,0:T(8,128)(2,1)} reshape(bf16[384,2048]{1,0:T(8,128)(2,1)} %scatter_custom_fusion) | data formatting | bytes 3145728 | tf_op jit(solution)/shard_map/reshape | solution.py:149
  65.3 3.2 %copy.96 = bf16[32,2,6,2048]{3,1,2,0:T(2,128)(2,1)S(1)} copy(bf16[32,2,6,2048]{3,2,1,0:T(8,128)(2,1)} %reshape.317) | data formatting | bytes 3145728 | tf_op jit(solution)/shard_map/reshape | solution.py:149
  68.5 37.2 %all_to_all.10 = bf16[32,2,6,2048]{3,1,2,0:T(2,128)(2,1)S(1)} all-to-all(bf16[32,2,6,2048]{3,1,2,0:T(2,128)(2,1)S(1)} %copy.96), channel_id=1, replica_groups=mesh['dp'=32,'head'=4] {'dp'}, dimensions={0} | all-to-all | bytes 3145728 | tf_op jit(solution)/shard_map/all_to_all | solution.py:148
  105.8 5.9 %fusion.15 = f32[32,2,6,2,352]{4,0,3,2,1:T(8,128)S(1)} fusion(bf16[2,2048,2,352]{1,3,2,0:T(8,128)(2,1)} %param.32, bf16[32,2,6,2048,1]{3,1,2,0,4:T(2,128)(2,1)S(1)} %bitcast.108), kind=kOutput, calls=%fused_computation.17 | convolution fusion | flops 1107296256 | bytes 8421376 | tf_op jit(solution)/shard_map/secd,edkf->seckf/dot_general | solution.py:155
  111.6 2.2 %fusion.11 = bf16[32,2,6,2048]{3,0,2,1:T(8,128)(2,1)} fusion(bf16[2,352,2048]{2,1,0:T(8,128)(2,1)S(1)} %copy-done.11, f32[32,2,6,2,352]{4,0,3,2,1:T(8,128)S(1)} %fusion.15), kind=kOutput, calls=%fused_computation.13 | convolution fusion | flops 555245568 | bytes 5537792 | tf_op jit(solution)/shard_map/secf,efd->secd/dot_general | solution.py:159
  113.9 2.9 %fusion.6 = f32[32,2,352]{2,0,1:T(8,128)S(1)} fusion(bf16[2048,2,352]{0,2,1:T(8,128)(2,1)} %param.34, bf16[32,2048]{1,0:T(8,128)(2,1)S(1)} %fusion.39), kind=kOutput, calls=%fused_computation.10 | convolution fusion | flops 92274688 | bytes 3104768 | tf_op jit(solution)/shard_map/dot_general | solution.py:176
  116.8 1.0 convolution_convert_fusion
  118.1 1.1 fusion.79
  119.2 1.6 gather_fusion.1
  121.1 14.4 %reduce-scatter.5.cloned.1.call-done = bf16[32,2,6,512]{3,0,2,1:T(8,128)(2,1)} async-done(((bf16[32,2,6,2048]{3,0,2,1:T(8,128)(2,1)}), bf16[32,2,6,512]{3,0,2,1:T(8,128)(2,1)}) %reduce-scatter.5.cloned.1.call-update) | async-done | bytes 393232 | tf_op jit(solution)/shard_map/reduce_scatter | solution.py:162
  135.4 2.1 %copy.99 = bf16[32,2,6,512]{3,1,2,0:T(2,128)(2,1)} copy(bf16[32,2,6,512]{3,0,2,1:T(8,128)(2,1)} %reduce-scatter.5.cloned.1.call-done) | data formatting | bytes 786432 | tf_op jit(solution)/shard_map/reduce_scatter | solution.py:162
  137.6 8.4 %all-to-all-start.1 = ((bf16[32,2,6,512]{3,1,2,0:T(2,128)(2,1)}), bf16[32,2,6,512]{3,1,2,0:T(2,128)(2,1)S(1)}, u32[]{:S(2)}, u32[]{:S(2)}) async-start(bf16[32,2,6,512]{3,1,2,0:T(2,128)(2,1)} %copy.99), calls=%async_computation.3 | async-start | bytes 786432 | tf_op jit(solution)/shard_map/all_to_all | solution.py:165
  146.1 0.6 multiply_divide_fusion
  146.7 0.8 copy.91
  147.4 1.3 pad_clamp_fusion
  148.7 7.5 %all-to-all-done.1 = bf16[32,2,6,512]{3,1,2,0:T(2,128)(2,1)S(1)} async-done(((bf16[32,2,6,512]{3,1,2,0:T(2,128)(2,1)}), bf16[32,2,6,512]{3,1,2,0:T(2,128)(2,1)S(1)}, u32[]{:S(2)}, u32[]{:S(2)}) %all-to-all-start.1) | async-done | bytes 393248 | tf_op jit(solution)/shard_map/all_to_all | solution.py:165
  156.2 0.9 copy.100
  157.1 1.2 reshape.318
  158.3 1.8 %gather_fusion = bf16[192,512]{1,0:T(8,128)(2,1)} fusion(bf16[384,512]{1,0:T(8,128)(2,1)S(1)} %reshape.318, s32[1024]{0:T(1024)} %pad_clamp_fusion), kind=kCustom, calls=%fused_computation.1 | custom fusion | bytes 393984 | tf_op jit(solution)/shard_map/gather | solution.py:168
  160.1 1.8 %reshape.320 = f32[32,6,512]{2,1,0:T(8,128)} reshape(bf16[192,512]{1,0:T(8,128)(2,1)} %gather_fusion) | data formatting | bytes 589824 | tf_op jit(solution)/shard_map/convert_element_type | solution.py:168
  161.8 1.3 multiply_reduce_fusion
  163.1 1.4 add_convert_fusion
  (68 shorter events, 5.4 us)
Async XLA Ops:
  6.5 20.4 %copy-start = (bf16[2048,768]{1,0:T(8,128)(2,1)S(1)}, bf16[2048,768]{1,0:T(8,128)(2,1)}, u32[]{:S(2)}) copy-start(bf16[2048,768]{1,0:T(8,128)(2,1)} %param.20) | copy-start | bytes 9437188
  6.5 128.9 %reduce-scatter.5.cloned.1.call-start = ((), (), s32[]{:S(2)}) async-start(), calls=%async_computation.5 | async-start | bytes 1966080 | tf_op jit(solution)/shard_map/reduce_scatter | solution.py:162
  37.2 3.8 %copy-start.1 = (bf16[32,128,576]{1,2,0:T(8,128)(2,1)S(1)}, bf16[32,128,576]{1,2,0:T(8,128)(2,1)}, u32[]{:S(2)}) copy-start(bf16[32,128,576]{1,2,0:T(8,128)(2,1)} %param.26) | copy-start | bytes 14155780
  40.9 1.2 copy-start.6
  40.9 1.8 %copy-start.3 = (bf16[512,2048]{1,0:T(8,128)(2,1)S(1)}, bf16[512,2048]{1,0:T(8,128)(2,1)}, u32[]{:S(2)}) copy-start(bf16[512,2048]{1,0:T(8,128)(2,1)} %param.25) | copy-start | bytes 6291460
  42.2 12.8 %copy-start.2 = (bf16[32,2048]{1,0:T(8,128)(2,1)S(1)}, bf16[32,2048]{1,0:T(8,128)(2,1)}, u32[]{:S(2)}) copy-start(bf16[32,2048]{1,0:T(8,128)(2,1)} %param.18) | copy-start | bytes 393220
  42.7 12.4 %copy-start.9 = (pred[192,1]{0,1:T(4,128)(4,1)S(1)}, pred[192,1]{0,1:T(4,128)(4,1)}, u32[]{:S(2)}) copy-start(pred[192,1]{0,1:T(4,128)(4,1)} %eq.57) | copy-start | bytes 580
  42.7 12.4 %copy-start.10 = (s32[192,1]{0,1:T(1,128)S(1)}, s32[192,1]{0,1:T(1,128)}, u32[]{:S(2)}) copy-start(s32[192,1]{0,1:T(1,128)} %mul.265) | copy-start | bytes 2308
  42.7 13.0 %copy-start.8 = (f32[2048]{0:T(1024)S(1)}, f32[2048]{0:T(1024)}, u32[]{:S(2)}) copy-start(f32[2048]{0:T(1024)} %param.29) | copy-start | bytes 24580
  55.1 0.6 copy-start.5
  105.8 5.9 %copy-start.11 = (bf16[2,352,2048]{2,1,0:T(8,128)(2,1)S(1)}, bf16[2,352,2048]{2,1,0:T(8,128)(2,1)}, u32[]{:S(2)}) copy-start(bf16[2,352,2048]{2,1,0:T(8,128)(2,1)} %param.33) | copy-start | bytes 8650756
  113.8 4.0 %copy-start.7 = (s32[32,6]{0,1:T(8,128)S(1)}, s32[32,6]{0,1:T(8,128)}, u32[]{:S(2)}) copy-start(s32[32,6]{0,1:T(8,128)} %param.31) | copy-start | bytes 2308
  113.8 49.3 %reduce-scatter.3.cloned.1.call-start = ((), (), s32[]{:S(2)}) async-start(), calls=%async_computation.4 | async-start | bytes 163840 | tf_op jit(solution)/shard_map/reduce_scatter | solution.py:183
  113.9 2.9 %copy-start.4 = (bf16[352,2048]{1,0:T(8,128)(2,1)S(1)}, bf16[352,2048]{1,0:T(8,128)(2,1)}, u32[]{:S(2)}) copy-start(bf16[352,2048]{1,0:T(8,128)(2,1)} %param.35) | copy-start | bytes 4325380
  119.2 26.8 %copy-start.12 = (s32[32]{0:T(128)S(1)}, s32[32]{0:T(128)}, u32[]{:S(2)}) copy-start(s32[32]{0:T(128)} %param.28) | copy-start | bytes 388
  137.6 18.6 %all-to-all-start.1 = ((bf16[32,2,6,512]{3,1,2,0:T(2,128)(2,1)}), bf16[32,2,6,512]{3,1,2,0:T(2,128)(2,1)S(1)}, u32[]{:S(2)}, u32[]{:S(2)}) async-start(bf16[32,2,6,512]{3,1,2,0:T(2,128)(2,1)} %copy.99), calls=%async_computation.3 | async-start | bytes 786432 | tf_op jit(solution)/shard_map/all_to_all | solution.py:165
Sparse Core Ops, SparseCore 0:
  114.0 21.4 reduce-scatter.4
  137.8 19.2 reduce-scatter.2
